TPU v7x, 512 devices: a whole 4x4x16 slice. The times are simulated.
512 devices in a mesh: seq: 64 (over y, z), req: 8 (over x, core).
Axes of the slice: x: 4, y: 4, z: 16, core: 2. Of those that a mesh axis runs over, the one named last changes fastest.
Arguments:
- new_token_queries: bfloat16 [4, 64, 2048], P(None, 'req'), may hold values from -48 to 48
- new_token_keys: bfloat16 [4, 64, 1024], P(None, 'req'), may hold values from -48 to 48
- new_token_values: bfloat16 [4, 64, 1024], P(None, 'req'), may hold values from -6 to 6
- key_cache: bfloat16 [64, 2048, 1024], P('req', 'seq'), may hold values from -48 to 48
- value_cache: bfloat16 [64, 2048, 1024], P('req', 'seq'), may hold values from -6 to 6
- cache_len: int32 [64], P('req'), may hold values from 1 to 2048, 34816 in all
- resid: bfloat16 [4, 64, 2048], P(None, 'req'), may hold values from -6 to 6
- gain: bfloat16 [2048], replicated, may hold values from 0.5 to 1.5
- w_gate: bfloat16 [2048, 6144], P('seq', 'req'), may hold values from -0.125 to 0.125
- w_up: bfloat16 [2048, 6144], P('seq', 'req'), may hold values from -0.125 to 0.125
- w_down: bfloat16 [6144, 2048], P('req', 'seq'), may hold values from -0.078125 to 0.078125
Outputs:
- out: bfloat16 [4, 64, 2048], P(None, 'req')
All inputs are finite; a program needn't handle non-finite values. No bound on the sum of `cache_len` on one device may be relied on, other than what follows from the above.
Results may differ from a plain program's by a relative error of at most 0.006.
Values may be sent and summed in bfloat16 or wider, within the bound.
A program may use at most 128 MiB of HBM per device.

v0:
```python
import math
import jax
import jax.numpy as jnp
from jax import lax
from jax.sharding import PartitionSpec as P

QUERY_HEADS = 16
KEY_VALUE_HEADS = 8
HEAD_SIZE = 128
DECODE_STEPS = 4
NEG_FILL = -1e30
EPSILON = 1e-06


def page_partial(query_vector, key_row_set, value_row_set, valid):
    scores = jnp.einsum(
        "rkgd,rbkd->rkgb", query_vector, key_row_set, preferred_element_type=jnp.float32
    ) / math.sqrt(HEAD_SIZE)
    inside = valid[:, None, None, :]
    scores = jnp.where(inside, scores, NEG_FILL)
    highest = jnp.max(scores, axis=-1)
    weights = jnp.where(inside, jnp.exp(scores - highest[..., None]), 0.0).astype(jnp.bfloat16)
    totals = jnp.sum(weights.astype(jnp.float32), axis=-1)
    weighted = jnp.einsum(
        "rkgb,rbkd->rkgd", weights, value_row_set, preferred_element_type=jnp.float32
    )
    return (highest, totals, weighted)


def merge_pair(former, latter):
    highest = jnp.maximum(former[0], latter[0])
    first_scale = jnp.exp(former[0] - highest)
    second_scale = jnp.exp(latter[0] - highest)
    totals = first_scale * former[1] + second_scale * latter[1]
    weighted = first_scale[..., None] * former[2] + second_scale[..., None] * latter[2]
    return (highest, totals, weighted)


def body(
    new_token_queries,
    new_token_keys,
    new_token_values,
    key_cache,
    value_cache,
    cache_len,
    resid,
    gain,
    w_gate,
    w_up,
    w_down,
):
    count_of_rows = new_token_queries.shape[1]
    page_length = key_cache.shape[1]
    head_cluster = QUERY_HEADS // KEY_VALUE_HEADS
    slice_width = w_gate.shape[0]
    unit_count = w_gate.shape[1]
    seq_index = lax.axis_index("seq")
    positions = seq_index * page_length + jnp.arange(page_length, dtype=jnp.int32)
    valid = positions[None, :] < cache_len[:, None]
    key_row_set = key_cache.reshape(count_of_rows, page_length, KEY_VALUE_HEADS, HEAD_SIZE)
    value_row_set = value_cache.reshape(count_of_rows, page_length, KEY_VALUE_HEADS, HEAD_SIZE)
    joined = jnp.concatenate([w_gate, w_up], axis=1)
    gain_scale = gain.astype(jnp.float32)
    results = []
    for decode_step_index in range(DECODE_STEPS):
        query_vector = new_token_queries[decode_step_index].reshape(
            count_of_rows, KEY_VALUE_HEADS, head_cluster, HEAD_SIZE
        )
        local = page_partial(query_vector, key_row_set, value_row_set, valid)
        highest = lax.pmax(local[0], "seq")
        factor = jnp.exp(local[0] - highest)
        totals, weighted = lax.psum((factor * local[1], factor[..., None] * local[2]), "seq")
        incoming_keys = jnp.swapaxes(new_token_keys[: decode_step_index + 1], 0, 1).reshape(
            count_of_rows, decode_step_index + 1, KEY_VALUE_HEADS, HEAD_SIZE
        )
        incoming_values = jnp.swapaxes(new_token_values[: decode_step_index + 1], 0, 1).reshape(
            count_of_rows, decode_step_index + 1, KEY_VALUE_HEADS, HEAD_SIZE
        )
        fresh_valid = jnp.ones((count_of_rows, decode_step_index + 1), jnp.bool_)
        fresh = page_partial(query_vector, incoming_keys, incoming_values, fresh_valid)
        combined = merge_pair((highest, totals, weighted), fresh)
        attention = (
            (combined[2] / combined[1][..., None])
            .reshape(count_of_rows, QUERY_HEADS * HEAD_SIZE)
            .astype(jnp.bfloat16)
        )
        attention = lax.optimization_barrier(attention).astype(jnp.float32)
        stream = (resid[decode_step_index].astype(jnp.float32) + attention).astype(jnp.bfloat16)
        stream = lax.optimization_barrier(stream).astype(jnp.float32)
        scaled = lax.rsqrt(jnp.mean(stream * stream, axis=-1, keepdims=True) + EPSILON)
        normed = (stream * scaled * gain_scale).astype(jnp.bfloat16)
        own_slice = lax.dynamic_slice_in_dim(normed, seq_index * slice_width, slice_width, 1)
        partial_sums = jnp.dot(
            lax.all_gather(own_slice, "req", axis=0, tiled=True),
            joined,
            preferred_element_type=jnp.float32,
        )
        whole_sums = lax.psum(partial_sums, "seq")
        hidden = (jax.nn.silu(whole_sums[:, :unit_count]) * whole_sums[:, unit_count:]).astype(
            jnp.bfloat16
        )
        down_sum = lax.psum_scatter(
            jnp.dot(hidden, w_down, preferred_element_type=jnp.float32),
            "req",
            scatter_dimension=0,
            tiled=True,
        )
        stream_slice = lax.dynamic_slice_in_dim(stream, seq_index * slice_width, slice_width, 1)
        out_piece = (stream_slice + down_sum).astype(jnp.bfloat16)
        results.append(lax.all_gather(out_piece, "seq", axis=1, tiled=True))
    return jnp.stack(results)


def solution(mesh):
    placed = (
        P(None, "req", None),
        P(None, "req", None),
        P(None, "req", None),
        P("req", "seq", None),
        P("req", "seq", None),
        P("req"),
        P(None, "req", None),
        P(),
        P("seq", "req"),
        P("seq", "req"),
        P("req", "seq"),
    )
    return jax.shard_map(
        body, mesh=mesh, in_specs=placed, out_specs=P(None, "req", None), check_vma=False
    )
```

profile of v0, /device:TPU:8, one launch (start us, length us, event | category | flops | bytes accessed | tf_op | source)
XLA Modules:
  0.0 1327.7 jit_solution(7573360003918362906)
XLA Ops:
  6.5 0.9 fusion.88
  8.2 1.5 fusion.89
  11.1 261.7 %all-reduce.7 = (f32[8,8,2]{2,1,0:T(8,128)S(1)}, f32[8,8,2]{2,1,0:T(8,128)S(1)}, f32[8,8,2]{2,1,0:T(8,128)S(1)}, f32[8,8,2]{2,1,0:T(8,128)S(1)}) all-reduce(f32[8,8,2]{2,1,0:T(8,128)S(1)} %get-tuple-element.80, f32[8,8,2]{2,1,0:T(8,128)S(1)} %get-tuple-element.78, ...), channel_id=1, replica_groups=mesh['seq'=64,'req'=8] {'seq'}, use_global_device_ids=true, to_apply=%region_29.30 | all-reduce | flops 512 | bytes 4096 | tf_op jit(solution)/shard_map/pmax | solution.py:70
  273.5 0.9 convolution_multiply_fusion.11
  274.4 0.9 convolution_multiply_fusion.9
  275.3 0.9 convolution_multiply_fusion.7
  276.2 0.9 convolution_multiply_fusion.5
  280.1 274.1 %all-reduce.4 = (f32[8,8,2]{2,1,0:T(8,128)S(1)}, f32[8,8,2]{2,1,0:T(8,128)S(1)}, f32[8,8,2]{2,1,0:T(8,128)S(1)}, f32[8,8,2]{2,1,0:T(8,128)S(1)}) all-reduce(f32[8,8,2]{2,1,0:T(8,128)S(1)} %get-tuple-element.88, f32[8,8,2]{2,1,0:T(8,128)S(1)} %get-tuple-element.47, ...), channel_id=1, replica_groups=mesh['seq'=64,'req'=8] {'seq'}, use_global_device_ids=true, to_apply=%region_33.34 | all-reduce | flops 512 | bytes 4096 | tf_op jit(solution)/shard_map/psum | solution.py:72
  554.5 0.8 copy-done.6
  555.7 0.8 dynamic-slice.8
  556.6 1.2 fusion.11
  557.8 0.8 copy-done.13
  559.0 0.8 copy-done.12
  560.1 0.8 copy-done.4
  562.6 12.0 all_gather.24
  574.6 11.2 all_gather.26
  585.8 0.9 fusion.95
  586.8 0.9 fusion.96
  587.7 11.3 all_gather.28
  599.0 0.9 fusion.97
  599.9 11.2 all_gather.30
  611.2 0.9 fusion.98
  612.1 1.3 dynamic-slice
  614.0 286.2 %all-reduce.12.cloned.1.call-done = (f32[64,1536]{1,0:T(8,128)}, f32[64,1536]{1,0:T(8,128)}, f32[64,1536]{1,0:T(8,128)}, f32[64,1536]{1,0:T(8,128)}) async-done(((f32[64,1536]{1,0:T(8,128)}, f32[64,1536]{1,0:T(8,128)}, f32[64,1536]{1,0:T(8,128)}, f32[64,1536]{1,0:T(8,128)}), (f32[64,1536]{1,0:T(8,128)}, f32[64,1536]{1,0:T(8,128)}, f32[64,1536]{1,0:T(8,128)}, ...) | async-done | bytes 1572880 | tf_op jit(solution)/shard_map/psum | solution.py:98
  900.2 1.2 fusion.33
  901.7 0.8 copy-done.10
  902.7 0.8 copy-done.9
  903.7 24.8 %all-reduce.8 = (f32[64,32]{1,0:T(8,128)S(1)}, f32[64,32]{1,0:T(8,128)S(1)}, f32[64,32]{1,0:T(8,128)S(1)}, f32[64,32]{1,0:T(8,128)S(1)}) all-reduce(f32[64,32]{1,0:T(8,128)S(1)} %fusion.39, f32[64,32]{1,0:T(8,128)S(1)} %fusion.37, f32[64,32]{1,0:T(8,128)S(1)} %fusion.35, ...), channel_id=5, replica_groups=mesh['seq'=64,'req'=8] {'req'}, use_global_device_ids=true, to_apply=%region_37.38.clone | all-reduce | flops 8192 | bytes 65536
  928.6 97.9 %all-gather = bf16[64,32,8]{1,2,0:T(8,128)(2,1)S(1)} all-gather(bf16[1,32,8]{1,2,0:T(8,128)(2,1)S(1)} %fusion.68), channel_id=1, replica_groups=mesh['seq'=64,'req'=8] {'seq'}, dimensions={0}, use_global_device_ids=true | all-gather | bytes 33280 | tf_op jit(solution)/shard_map/all_gather | solution.py:110
  1026.8 97.5 %all-gather.1 = bf16[64,32,8]{1,2,0:T(8,128)(2,1)S(1)} all-gather(bf16[1,32,8]{1,2,0:T(8,128)(2,1)S(1)} %fusion.69), channel_id=1, replica_groups=mesh['seq'=64,'req'=8] {'seq'}, dimensions={0}, use_global_device_ids=true | all-gather | bytes 33280 | tf_op jit(solution)/shard_map/all_gather | solution.py:110
  1124.5 97.6 %all-gather.2 = bf16[64,32,8]{1,2,0:T(8,128)(2,1)S(1)} all-gather(bf16[1,32,8]{1,2,0:T(8,128)(2,1)S(1)} %fusion.70), channel_id=1, replica_groups=mesh['seq'=64,'req'=8] {'seq'}, dimensions={0}, use_global_device_ids=true | all-gather | bytes 33280 | tf_op jit(solution)/shard_map/all_gather | solution.py:110
  1222.5 97.5 %all-gather.3 = bf16[64,32,8]{1,2,0:T(8,128)(2,1)S(1)} all-gather(bf16[1,32,8]{1,2,0:T(8,128)(2,1)S(1)} %fusion.71), channel_id=1, replica_groups=mesh['seq'=64,'req'=8] {'seq'}, dimensions={0}, use_global_device_ids=true | all-gather | bytes 33280 | tf_op jit(solution)/shard_map/all_gather | solution.py:110
  (107 shorter events, 11.2 us)
Async XLA Ops:
  6.5 267.0 %copy-start = (bf16[8,32,1024]{2,1,0:T(8,128)(2,1)S(1)}, bf16[8,32,1024]{2,1,0:T(8,128)(2,1)}, u32[]{:S(2)}) copy-start(bf16[8,32,1024]{2,1,0:T(8,128)(2,1)} %param.15) | copy-start | bytes 1572868
  6.5 550.0 %all-reduce.14.cloned.1.call-start = ((), (), s32[]{:S(2)}) async-start(), calls=%async_computation.1 | async-start | bytes 524288 | tf_op jit(solution)/shard_map/psum | solution.py:72
  7.4 0.7 copy-start.7
  7.5 2.2 copy-start.8
  277.0 0.8 copy-start.1
  277.1 0.9 copy-start.2
  277.1 623.2 %all-reduce.12.cloned.1.call-start = ((), (), s32[]{:S(2)}) async-start(), calls=%async_computation | async-start | bytes 3145728 | tf_op jit(solution)/shard_map/psum | solution.py:98
  279.0 0.8 copy-start.5
  554.5 0.8 copy-start.6
  557.8 0.8 copy-start.13
  559.0 0.8 copy-start.12
  560.1 0.8 copy-start.4
  561.0 0.9 copy-start.3
  612.1 288.2 %copy-start.14 = (bf16[768,32]{0,1:T(8,128)(2,1)S(1)}, bf16[768,32]{0,1:T(8,128)(2,1)}, u32[]{:S(2)}) copy-start(bf16[768,32]{0,1:T(8,128)(2,1)} %param.21) | copy-start | bytes 147460
  900.2 1.3 copy-start.11
  901.5 1.0 copy-start.10
  902.5 1.0 copy-start.9
Sparse Core Ops, SparseCore 0:
  277.2 274.5 all-reduce.13
  612.2 287.9 all-reduce.11
where the time goes:
time: 1330 us
  blocking collectives  997 us (75%)
  waiting for transfers between devices  286 us (22%)
  matrix products  14.7 us (1%)
  between operations  14.5 us (1%)
    all_gather x4, blocking collectives, body(): results.append(lax.all_gather(out_piece, 'seq', axis=1, tiled=True))  391 us
    psum x1, waiting for transfers between devices, body(): whole_sums = lax.psum(partial_sums, 'seq')  286 us
    psum x1, blocking collectives, body(): lax.psum((factor * local[1], factor[..., None] * local[2]), 'seq')  274 us
    pmax x1, blocking collectives, body(): highest = lax.pmax(local[0], 'seq')  262 us
    all_gather x4, blocking collectives, body(): lax.all_gather(own_slice, 'req', axis=0, tiled=True)  45.8 us
  transfers between devices with their start and end apart: 2, of which 1 were waited for; matrix products, arithmetic and copies ran while one was open for 0% of the time, Pallas kernels for 0%

commit v1 on v0

--- a/solution.py
+++ b/solution.py
@@ -95,7 +95,7 @@
             joined,
             preferred_element_type=jnp.float32,
         )
-        whole_sums = lax.psum(partial_sums, "seq")
+        whole_sums = jnp.sum(lax.all_gather(partial_sums, "seq"), axis=0)
         hidden = (jax.nn.silu(whole_sums[:, :unit_count]) * whole_sums[:, unit_count:]).astype(
             jnp.bfloat16
         )

time: 1330 us -> 2010 us (1.51)
  the two profiles are of different devices: /device:TPU:8 before, /device:TPU:32 now
where the time goes in v1:
time: 2010 us
  blocking collectives  1020 us (51%)
  waiting for transfers between devices  897 us (45%)
  other arithmetic  44.2 us (2%)
    all_gather x4, waiting for transfers between devices, body(): whole_sums = jnp.sum(lax.all_gather(partial_sums, 'seq'), axis=0)  897 us
    all_gather x4, blocking collectives, body(): results.append(lax.all_gather(out_piece, 'seq', axis=1, tiled=True))  392 us
    pmax x1, blocking collectives, body(): highest = lax.pmax(local[0], 'seq')  280 us
    psum x1, blocking collectives, body(): lax.psum((factor * local[1], factor[..., None] * local[2]), 'seq')  276 us
    all_gather x4, blocking collectives, body(): lax.all_gather(own_slice, 'req', axis=0, tiled=True)  45.7 us
  transfers between devices with their start and end apart: 5, of which 4 were waited for; matrix products, arithmetic and copies ran while one was open for 2% of the time, Pallas kernels for 0%

profile of v1, /device:TPU:32, one launch (start us, length us, event | category | flops | bytes accessed | tf_op | source)
XLA Modules:
  0.0 2006.5 jit_solution(17208133815654008652)
XLA Ops:
  8.2 1.5 fusion.89
  9.7 1.5 fusion.90
  11.2 1.5 fusion.91
  12.8 1.5 fusion.92
  14.3 280.4 %all-reduce.6 = (f32[8,8,2]{2,1,0:T(8,128)S(1)}, f32[8,8,2]{2,1,0:T(8,128)S(1)}, f32[8,8,2]{2,1,0:T(8,128)S(1)}, f32[8,8,2]{2,1,0:T(8,128)S(1)}) all-reduce(f32[8,8,2]{2,1,0:T(8,128)S(1)} %get-tuple-element.76, f32[8,8,2]{2,1,0:T(8,128)S(1)} %get-tuple-element.74, ...), channel_id=1, replica_groups=mesh['seq'=64,'req'=8] {'seq'}, use_global_device_ids=true, to_apply=%region_29.30 | all-reduce | flops 512 | bytes 4096 | tf_op jit(solution)/shard_map/pmax | solution.py:70
  303.9 1.1 fusion.93
  306.7 276.4 %all-reduce.4 = (f32[8,8,2]{2,1,0:T(8,128)S(1)}, f32[8,8,2]{2,1,0:T(8,128)S(1)}, f32[8,8,2]{2,1,0:T(8,128)S(1)}, f32[8,8,2]{2,1,0:T(8,128)S(1)}) all-reduce(f32[8,8,2]{2,1,0:T(8,128)S(1)} %get-tuple-element.84, f32[8,8,2]{2,1,0:T(8,128)S(1)} %get-tuple-element.43, ...), channel_id=1, replica_groups=mesh['seq'=64,'req'=8] {'seq'}, use_global_device_ids=true, to_apply=%region_33.34 | all-reduce | flops 512 | bytes 4096 | tf_op jit(solution)/shard_map/psum | solution.py:72
  585.6 1.2 fusion.11
  586.8 1.2 fusion.12
  588.1 1.1 fusion.10
  589.3 1.2 fusion.45
  592.0 11.9 all_gather.48
  604.9 11.2 all_gather.52
  616.1 1.0 fusion.96
  617.2 11.3 all_gather.56
  628.5 0.9 fusion.97
  629.5 11.2 all_gather.60
  640.7 0.9 fusion.98
  641.7 1.3 dynamic-slice
  643.6 193.7 %all-gather.13.cloned.1.call-done = f32[4096,1536]{1,0:T(8,128)} async-done(((f32[64,1536]{1,0:T(8,128)}), f32[4096,1536]{1,0:T(8,128)}) %all-gather.13.cloned.1.call-update) | async-done | bytes 25165840 | tf_op jit(solution)/shard_map/all_gather | solution.py:98
  837.3 9.4 reduce_sum.141
  846.8 234.8 %all-gather.15.cloned.1.call-done = f32[4096,1536]{1,0:T(8,128)} async-done(((f32[64,1536]{1,0:T(8,128)}), f32[4096,1536]{1,0:T(8,128)}) %all-gather.15.cloned.1.call-update) | async-done | bytes 25165840 | tf_op jit(solution)/shard_map/all_gather | solution.py:98
  1081.6 9.4 reduce_sum.145
  1091.0 234.6 %all-gather.17.cloned.1.call-done = f32[4096,1536]{1,0:T(8,128)} async-done(((f32[64,1536]{1,0:T(8,128)}), f32[4096,1536]{1,0:T(8,128)}) %all-gather.17.cloned.1.call-update) | async-done | bytes 25165840 | tf_op jit(solution)/shard_map/all_gather | solution.py:98
  1325.6 9.5 reduce_sum.149
  1335.7 234.0 %all-gather.19.cloned.1.call-done = f32[4096,1536]{1,0:T(8,128)} async-done(((f32[64,1536]{1,0:T(8,128)}), f32[4096,1536]{1,0:T(8,128)}) %all-gather.19.cloned.1.call-update) | async-done | bytes 25165840 | tf_op jit(solution)/shard_map/all_gather | solution.py:98
  1569.7 9.4 reduce_sum.153
  1579.3 26.5 %all-reduce.7 = (f32[64,32]{1,0:T(8,128)S(1)}, f32[64,32]{1,0:T(8,128)S(1)}, f32[64,32]{1,0:T(8,128)S(1)}, f32[64,32]{1,0:T(8,128)S(1)}) all-reduce(f32[64,32]{1,0:T(8,128)S(1)} %fusion.39, f32[64,32]{1,0:T(8,128)S(1)} %fusion.37, f32[64,32]{1,0:T(8,128)S(1)} %fusion.35, ...), channel_id=9, replica_groups=mesh['seq'=64,'req'=8] {'req'}, use_global_device_ids=true, to_apply=%region_37.38.clone | all-reduce | flops 8192 | bytes 65536
  1605.9 99.1 %all-gather.4 = bf16[64,32,8]{1,2,0:T(8,128)(2,1)S(1)} all-gather(bf16[1,32,8]{1,2,0:T(8,128)(2,1)S(1)} %fusion.68), channel_id=1, replica_groups=mesh['seq'=64,'req'=8] {'seq'}, dimensions={0}, use_global_device_ids=true | all-gather | bytes 33280 | tf_op jit(solution)/shard_map/all_gather | solution.py:110
  1705.3 98.1 %all-gather.5 = bf16[64,32,8]{1,2,0:T(8,128)(2,1)S(1)} all-gather(bf16[1,32,8]{1,2,0:T(8,128)(2,1)S(1)} %fusion.69), channel_id=1, replica_groups=mesh['seq'=64,'req'=8] {'seq'}, dimensions={0}, use_global_device_ids=true | all-gather | bytes 33280 | tf_op jit(solution)/shard_map/all_gather | solution.py:110
  1803.7 97.1 %all-gather.6 = bf16[64,32,8]{1,2,0:T(8,128)(2,1)S(1)} all-gather(bf16[1,32,8]{1,2,0:T(8,128)(2,1)S(1)} %fusion.70), channel_id=1, replica_groups=mesh['seq'=64,'req'=8] {'seq'}, dimensions={0}, use_global_device_ids=true | all-gather | bytes 33280 | tf_op jit(solution)/shard_map/all_gather | solution.py:110
  1901.0 98.1 %all-gather.7 = bf16[64,32,8]{1,2,0:T(8,128)(2,1)S(1)} all-gather(bf16[1,32,8]{1,2,0:T(8,128)(2,1)S(1)} %fusion.71), channel_id=1, replica_groups=mesh['seq'=64,'req'=8] {'seq'}, dimensions={0}, use_global_device_ids=true | all-gather | bytes 33280 | tf_op jit(solution)/shard_map/all_gather | solution.py:110
  (96 shorter events, 20.1 us)
Async XLA Ops:
  6.5 288.9 %copy-start = (bf16[8,32,1024]{2,1,0:T(8,128)(2,1)S(1)}, bf16[8,32,1024]{2,1,0:T(8,128)(2,1)}, u32[]{:S(2)}) copy-start(bf16[8,32,1024]{2,1,0:T(8,128)(2,1)} %param.15) | copy-start | bytes 1572868
  6.5 579.0 %all-reduce.10.cloned.1.call-start = ((), (), s32[]{:S(2)}) async-start(), calls=%async_computation.4 | async-start | bytes 524288 | tf_op jit(solution)/shard_map/psum | solution.py:72
  299.0 538.4 %all-gather.13.cloned.1.call-start = ((), (), s32[]{:S(2)}) async-start(), calls=%async_computation | async-start | bytes 25559040 | tf_op jit(solution)/shard_map/all_gather | solution.py:98
  604.8 476.7 %all-gather.15.cloned.1.call-start = ((), (), s32[]{:S(2)}) async-start(), calls=%async_computation.1 | async-start | bytes 25559040 | tf_op jit(solution)/shard_map/all_gather | solution.py:98
  617.1 708.5 %all-gather.17.cloned.1.call-start = ((), (), s32[]{:S(2)}) async-start(), calls=%async_computation.2 | async-start | bytes 25559040 | tf_op jit(solution)/shard_map/all_gather | solution.py:98
  629.4 940.3 %all-gather.19.cloned.1.call-start = ((), (), s32[]{:S(2)}) async-start(), calls=%async_computation.3 | async-start | bytes 25559040 | tf_op jit(solution)/shard_map/all_gather | solution.py:98
  1081.6 253.5 %copy-start.2 = (bf16[768,32]{0,1:T(8,128)(2,1)S(1)}, bf16[768,32]{0,1:T(8,128)(2,1)}, u32[]{:S(2)}) copy-start(bf16[768,32]{0,1:T(8,128)(2,1)} %param.21) | copy-start | bytes 147460
  1325.6 674.3 %copy-start.1 = (bf16[8,32,1024]{2,1,0:T(8,128)(2,1)S(1)}, bf16[8,32,1024]{2,1,0:T(8,128)(2,1)}, u32[]{:S(2)}) copy-start(bf16[8,32,1024]{2,1,0:T(8,128)(2,1)} %param.15) | copy-start | bytes 1572868
Sparse Core Ops, SparseCore 0:
  299.1 255.9 all-reduce.9
  605.0 232.3 all-gather.12
  840.7 240.7 all-gather.14
  1084.8 240.7 all-gather.16
  1328.8 240.7 all-gather.18
